TPU v7x, 32 devices: a whole 2x2x4 slice. The times are simulated.
32 devices in a mesh: dp: 8 (over z, x), tensor: 4 (over y, core).
Axes of the slice: x: 2, y: 2, z: 4, core: 2. Of those that a mesh axis runs over, the one named last changes fastest.
Arguments:
- hidden_in: float32 [4096, 1536], P('dp'), may hold values from -6 to 6
- doc_lengths: int32 [2, 2], replicated, may hold values from 1 to 1792, 2048 in all within a row
- norm_attn: float32 [2, 1536], replicated, may hold values from 0.5 to 1.5
- norm_mlp: float32 [2, 1536], replicated, may hold values from 0.5 to 1.5
- w_query: bfloat16 [2, 1536, 1536], P(None, None, 'tensor'), may hold values from -0.15625 to 0.15625
- w_key: bfloat16 [2, 1536, 768], P(None, None, 'tensor'), may hold values from -0.15625 to 0.15625
- w_value: bfloat16 [2, 1536, 768], P(None, None, 'tensor'), may hold values from -0.15625 to 0.15625
- w_out: bfloat16 [2, 1536, 1536], P(None, 'tensor'), may hold values from -0.625 to 0.625
- w_gate: bfloat16 [2, 1536, 4096], P(None, None, 'tensor'), may hold values from -0.15625 to 0.15625
- w_up: bfloat16 [2, 1536, 4096], P(None, None, 'tensor'), may hold values from -0.15625 to 0.15625
- w_down: bfloat16 [2, 4096, 1536], P(None, 'tensor'), may hold values from -0.09375 to 0.09375
- cotangent: float32 [4096, 1536], P('dp'), may hold values from -6 to 6
Outputs:
- hidden_out: float32 [4096, 1536], P('dp')
- input_grad: float32 [4096, 1536], P('dp')
- norm_attn_grad: float32 [2, 1536], P(None, 'dp')
- norm_mlp_grad: float32 [2, 1536], P(None, 'dp')
- w_query_grad: float32 [2, 1536, 1536], P(None, 'dp', 'tensor')
- w_key_grad: float32 [2, 1536, 768], P(None, 'dp', 'tensor')
- w_value_grad: float32 [2, 1536, 768], P(None, 'dp', 'tensor')
- w_out_grad: float32 [2, 1536, 1536], P(None, 'tensor', 'dp')
- w_gate_grad: float32 [2, 1536, 4096], P(None, 'dp', 'tensor')
- w_up_grad: float32 [2, 1536, 4096], P(None, 'dp', 'tensor')
- w_down_grad: float32 [2, 4096, 1536], P(None, 'tensor', 'dp')
Inputs may be any that keep to these rules, and one draw needn't show every extreme that they name: `doc_lengths`: each row holds 2 document lengths that add up to 2048, each at most 1792.
All inputs are finite; a program needn't handle non-finite values.
Results may differ from a plain program's by a relative error of at most 0.028.
Values may be sent and summed in bfloat16 or wider, within the bound.
No kernel may reach another device: no remote copies, remote signals or barrier semaphores. Data moves between devices by JAX's collectives and lax.ppermute only.
A program may use at most 320 MiB of HBM per device.

v0:
```python
import jax
import jax.numpy as jnp
from jax import lax
from jax.sharding import PartitionSpec as P

HD = 96
LAYERS = 2
STRETCHES = 4
EPS = 1e-05
BASE = 100000.0


def passed_along(block, axis, distance):
    devices = range(lax.axis_size(axis))
    route = [((i - distance) % len(devices), i) for i in devices]
    return lax.ppermute(block, axis, route)


def rope_tables(positions):
    half_dim = HD // 2
    frequency = BASE ** (-(jnp.arange(half_dim, dtype=jnp.float32) * 2.0 / HD))
    angles = positions.astype(jnp.float32)[:, None] * frequency[None, :]
    angles = jnp.concatenate([angles, angles], axis=1)
    return (jnp.cos(angles)[:, None, :], jnp.sin(angles)[:, None, :])


def rotate(values, cosine, sine_table):
    half_dim = values.shape[-1] // 2
    turned = jnp.concatenate([-values[..., half_dim:], values[..., :half_dim]], axis=-1)
    return values * cosine + turned * sine_table


def unrotate(gradient, cosine, sine_table):
    half_dim = gradient.shape[-1] // 2
    scaled_values = gradient * sine_table
    turned = jnp.concatenate(
        [scaled_values[..., half_dim:], -scaled_values[..., :half_dim]], axis=-1
    )
    return gradient * cosine + turned


def doc_place(places, lengths):
    doc_ends = jnp.cumsum(lengths, axis=1)
    passed = (places[:, None] >= doc_ends).astype(jnp.int32)
    doc_ids = jnp.sum(passed, axis=1)
    starts = jnp.sum(passed * lengths, axis=1)
    return (doc_ids, places - starts)


def scores_of(queries, key_rows, allowed):
    scores = jnp.einsum(
        "qkgd,tkd->kgqt", queries, key_rows, preferred_element_type=jnp.float32
    ) * HD ** (-0.5)
    return jnp.where(allowed[None, None], scores, -jnp.inf)


def attention_forward(queries, key_rows, value_rows, allowed):
    scores = scores_of(queries, key_rows, allowed)
    row_top = jnp.max(scores, axis=-1, keepdims=True)
    log_total = row_top + jnp.log(jnp.sum(jnp.exp(scores - row_top), axis=-1, keepdims=True))
    attn_probs = jnp.exp(scores - log_total).astype(jnp.bfloat16)
    mixed_heads = jnp.einsum(
        "kgqt,tkd->qkgd", attn_probs, value_rows, preferred_element_type=jnp.float32
    )
    return (mixed_heads.astype(jnp.bfloat16), log_total)


def attention_backward(queries, key_rows, value_rows, allowed, log_total, mixed_grad):
    scores = scores_of(queries, key_rows, allowed)
    attn_probs = jnp.exp(scores - log_total)
    prob_grad = jnp.einsum(
        "qkgd,tkd->kgqt", mixed_grad, value_rows, preferred_element_type=jnp.float32
    )
    centre = jnp.sum(attn_probs * prob_grad, axis=-1, keepdims=True)
    score_grad = (attn_probs * (prob_grad - centre) * HD ** (-0.5)).astype(jnp.bfloat16)
    probs_bf = attn_probs.astype(jnp.bfloat16)
    value_grad = jnp.einsum(
        "kgqt,qkgd->tkd", probs_bf, mixed_grad, preferred_element_type=jnp.float32
    )
    query_grad = jnp.einsum(
        "kgqt,tkd->qkgd", score_grad, key_rows, preferred_element_type=jnp.float32
    )
    key_grad = jnp.einsum("kgqt,qkgd->tkd", score_grad, queries, preferred_element_type=jnp.float32)
    return (query_grad, key_grad, value_grad)


def norm_back(residual_stream, inverse_norm, gain, normalized_gradient, incoming_gradient):
    normalized_input = residual_stream * inverse_norm
    scaled_values = normalized_gradient * gain
    gain_gradient = jnp.sum(normalized_gradient * normalized_input, axis=0)
    residual_gradient = incoming_gradient + inverse_norm * (
        scaled_values
        - normalized_input * jnp.mean(scaled_values * normalized_input, axis=1, keepdims=True)
    )
    return (residual_gradient, gain_gradient)


def forward_layer(residual_stream, params, tables, allowed):
    gain_attn, gain_mlp, query_w, key_w, value_w, out_w, gate_w, up_w, down_w = params
    cosine, sine_table = tables
    row_count = residual_stream.shape[0]
    query_heads = query_w.shape[1] // HD
    kv_heads = key_w.shape[1] // HD
    inv_attn = lax.rsqrt(jnp.mean(residual_stream * residual_stream, axis=1, keepdims=True) + EPS)
    normed_attn = (residual_stream * inv_attn * gain_attn).astype(jnp.bfloat16)
    queries = jnp.dot(normed_attn, query_w, preferred_element_type=jnp.float32).reshape(
        row_count, query_heads, HD
    )
    queries = rotate(queries, cosine, sine_table).astype(jnp.bfloat16)
    key_rows = jnp.dot(normed_attn, key_w, preferred_element_type=jnp.float32).reshape(
        row_count, kv_heads, HD
    )
    key_rows = (
        rotate(key_rows, cosine, sine_table).astype(jnp.bfloat16).reshape(row_count, kv_heads * HD)
    )
    value_rows = jnp.dot(normed_attn, value_w, preferred_element_type=jnp.float32).astype(
        jnp.bfloat16
    )
    key_list = [key_rows]
    value_list = [value_rows]
    for distance in range(1, STRETCHES):
        moved_keys, moved_values = passed_along((key_rows, value_rows), "dp", distance)
        key_list.append(moved_keys)
        value_list.append(moved_values)
    all_keys = jnp.concatenate(key_list, axis=0).reshape(STRETCHES * row_count, kv_heads, HD)
    all_values = jnp.concatenate(value_list, axis=0).reshape(STRETCHES * row_count, kv_heads, HD)
    grouped = queries.reshape(row_count, kv_heads, query_heads // kv_heads, HD)
    mixed_heads, log_total = attention_forward(grouped, all_keys, all_values, allowed)
    mixed_heads = mixed_heads.reshape(row_count, query_heads * HD)
    head_part = jnp.dot(mixed_heads, out_w, preferred_element_type=jnp.float32)
    middle = residual_stream + lax.psum(head_part, "tensor")
    inv_mlp = lax.rsqrt(jnp.mean(middle * middle, axis=1, keepdims=True) + EPS)
    normed_mlp = (middle * inv_mlp * gain_mlp).astype(jnp.bfloat16)
    gate_pre = jnp.dot(normed_mlp, gate_w, preferred_element_type=jnp.float32)
    up_values = jnp.dot(normed_mlp, up_w, preferred_element_type=jnp.float32)
    activated = (jax.nn.silu(gate_pre) * up_values).astype(jnp.bfloat16)
    unit_part = jnp.dot(activated, down_w, preferred_element_type=jnp.float32)
    result = middle + lax.psum(unit_part, "tensor")
    record = (
        residual_stream,
        inv_attn,
        normed_attn,
        grouped,
        all_keys,
        all_values,
        log_total,
        mixed_heads,
        middle,
        inv_mlp,
        normed_mlp,
        gate_pre,
        up_values,
        activated,
    )
    return (record, result)


def backward_layer(grad_flow, record, params, tables, allowed):
    gain_attn, gain_mlp, query_w, key_w, value_w, out_w, gate_w, up_w, down_w = params
    (
        residual_stream,
        inv_attn,
        normed_attn,
        grouped,
        all_keys,
        all_values,
        log_total,
        mixed_heads,
        middle,
        inv_mlp,
        normed_mlp,
        gate_pre,
        up_values,
        activated,
    ) = record
    cosine, sine_table = tables
    row_count = residual_stream.shape[0]
    query_heads = query_w.shape[1] // HD
    kv_heads = key_w.shape[1] // HD
    down_in = grad_flow.astype(jnp.bfloat16)
    grad_down = jnp.dot(activated.T, down_in, preferred_element_type=jnp.float32)
    hidden_grad = jnp.dot(down_in, down_w.T, preferred_element_type=jnp.float32)
    sigmoid_gate = jax.nn.sigmoid(gate_pre)
    gate_grad = (
        hidden_grad * up_values * sigmoid_gate * (1.0 + gate_pre * (1.0 - sigmoid_gate))
    ).astype(jnp.bfloat16)
    up_grad = (hidden_grad * gate_pre * sigmoid_gate).astype(jnp.bfloat16)
    grad_gate = jnp.dot(normed_mlp.T, gate_grad, preferred_element_type=jnp.float32)
    grad_up = jnp.dot(normed_mlp.T, up_grad, preferred_element_type=jnp.float32)
    unit_back = jnp.dot(gate_grad, gate_w.T, preferred_element_type=jnp.float32) + jnp.dot(
        up_grad, up_w.T, preferred_element_type=jnp.float32
    )
    mlp_norm_grad = lax.psum(unit_back, "tensor")
    middle_grad, grad_gain_mlp = norm_back(middle, inv_mlp, gain_mlp, mlp_norm_grad, grad_flow)
    out_in = middle_grad.astype(jnp.bfloat16)
    grad_out = jnp.dot(mixed_heads.T, out_in, preferred_element_type=jnp.float32)
    mixed_grad = jnp.dot(out_in, out_w.T, preferred_element_type=jnp.float32).astype(jnp.bfloat16)
    mixed_grad = mixed_grad.reshape(row_count, kv_heads, query_heads // kv_heads, HD)
    query_grad, key_grad, value_grad = attention_backward(
        grouped, all_keys, all_values, allowed, log_total, mixed_grad
    )
    key_grad = key_grad.reshape(STRETCHES * row_count, kv_heads * HD)
    value_grad = value_grad.reshape(STRETCHES * row_count, kv_heads * HD)
    key_total = key_grad[:row_count]
    value_total = value_grad[:row_count]
    for distance in range(1, STRETCHES):
        key_piece = key_grad[distance * row_count : (distance + 1) * row_count]
        value_piece = value_grad[distance * row_count : (distance + 1) * row_count]
        moved_keys, moved_values = passed_along((key_piece, value_piece), "dp", -distance)
        key_total = key_total + moved_keys
        value_total = value_total + moved_values
    query_grad = (
        unrotate(query_grad.reshape(row_count, query_heads, HD), cosine, sine_table)
        .astype(jnp.bfloat16)
        .reshape(row_count, query_heads * HD)
    )
    key_total = (
        unrotate(key_total.reshape(row_count, kv_heads, HD), cosine, sine_table)
        .astype(jnp.bfloat16)
        .reshape(row_count, kv_heads * HD)
    )
    value_total = value_total.astype(jnp.bfloat16)
    grad_query = jnp.dot(normed_attn.T, query_grad, preferred_element_type=jnp.float32)
    grad_key = jnp.dot(normed_attn.T, key_total, preferred_element_type=jnp.float32)
    grad_value = jnp.dot(normed_attn.T, value_total, preferred_element_type=jnp.float32)
    head_back = jnp.dot(query_grad, query_w.T, preferred_element_type=jnp.float32)
    head_back = head_back + jnp.dot(key_total, key_w.T, preferred_element_type=jnp.float32)
    head_back = head_back + jnp.dot(value_total, value_w.T, preferred_element_type=jnp.float32)
    attn_norm_grad = lax.psum(head_back, "tensor")
    residual_gradient, grad_gain_attn = norm_back(
        residual_stream, inv_attn, gain_attn, attn_norm_grad, middle_grad
    )
    return (
        residual_gradient,
        (
            grad_gain_attn,
            grad_gain_mlp,
            grad_query,
            grad_key,
            grad_value,
            grad_out,
            grad_gate,
            grad_up,
            grad_down,
        ),
    )


def shards(
    hidden_in,
    doc_lengths,
    norm_attn,
    norm_mlp,
    w_query,
    w_key,
    w_value,
    w_out,
    w_gate,
    w_up,
    w_down,
    cotangent,
):
    row_count = hidden_in.shape[0]
    seq_count = lax.axis_size("dp") // STRETCHES
    shifted_index = lax.axis_index("dp") + STRETCHES // 2
    stretch_index = shifted_index % STRETCHES
    seq_index = shifted_index // STRETCHES % seq_count
    lengths = lax.dynamic_slice_in_dim(doc_lengths, seq_index, 1, 0)
    local_rows = jnp.arange(row_count, dtype=jnp.int32)
    query_place = stretch_index * row_count + local_rows
    query_doc, query_pos = doc_place(query_place, lengths)
    key_parts = []
    for distance in range(STRETCHES):
        key_parts.append((stretch_index - distance) * row_count + local_rows)
    key_place = jnp.concatenate(key_parts)
    key_doc = doc_place(key_place, lengths)[0]
    allowed = (
        (key_place[None, :] >= 0)
        & (key_place[None, :] <= query_place[:, None])
        & (key_doc[None, :] == query_doc[:, None])
    )
    tables = rope_tables(query_pos)
    records = []
    flowing = hidden_in
    for layer_index in range(LAYERS):
        params = (
            norm_attn[layer_index],
            norm_mlp[layer_index],
            w_query[layer_index],
            w_key[layer_index],
            w_value[layer_index],
            w_out[layer_index],
            w_gate[layer_index],
            w_up[layer_index],
            w_down[layer_index],
        )
        record, flowing = forward_layer(flowing, params, tables, allowed)
        records.append(record)
    grad_flow = cotangent
    collected = [None] * LAYERS
    for layer_index in reversed(range(LAYERS)):
        params = (
            norm_attn[layer_index],
            norm_mlp[layer_index],
            w_query[layer_index],
            w_key[layer_index],
            w_value[layer_index],
            w_out[layer_index],
            w_gate[layer_index],
            w_up[layer_index],
            w_down[layer_index],
        )
        grad_flow, layer_grads = backward_layer(
            grad_flow, records[layer_index], params, tables, allowed
        )
        collected[layer_index] = layer_grads
    stacked = tuple(
        (jnp.stack([member[position] for member in collected]) for position in range(9))
    )
    stacked = (
        lax.psum_scatter(
            stacked[0].astype(jnp.bfloat16), "dp", scatter_dimension=1, tiled=True
        ).astype(jnp.float32),
        lax.psum_scatter(
            stacked[1].astype(jnp.bfloat16), "dp", scatter_dimension=1, tiled=True
        ).astype(jnp.float32),
        lax.psum_scatter(
            stacked[2].astype(jnp.bfloat16), "dp", scatter_dimension=1, tiled=True
        ).astype(jnp.float32),
        lax.psum_scatter(
            stacked[3].astype(jnp.bfloat16), "dp", scatter_dimension=1, tiled=True
        ).astype(jnp.float32),
        lax.psum_scatter(
            stacked[4].astype(jnp.bfloat16), "dp", scatter_dimension=1, tiled=True
        ).astype(jnp.float32),
        lax.psum_scatter(
            stacked[5].astype(jnp.bfloat16), "dp", scatter_dimension=2, tiled=True
        ).astype(jnp.float32),
        lax.psum_scatter(
            stacked[6].astype(jnp.bfloat16), "dp", scatter_dimension=1, tiled=True
        ).astype(jnp.float32),
        lax.psum_scatter(
            stacked[7].astype(jnp.bfloat16), "dp", scatter_dimension=1, tiled=True
        ).astype(jnp.float32),
        lax.psum_scatter(
            stacked[8].astype(jnp.bfloat16), "dp", scatter_dimension=2, tiled=True
        ).astype(jnp.float32),
    )
    return (
        flowing,
        grad_flow,
        stacked[0],
        stacked[1],
        stacked[2],
        stacked[3],
        stacked[4],
        stacked[5],
        stacked[6],
        stacked[7],
        stacked[8],
    )


def solution(mesh):
    placed = (
        P("dp", None),
        P(),
        P(),
        P(),
        P(None, None, "tensor"),
        P(None, None, "tensor"),
        P(None, None, "tensor"),
        P(None, "tensor", None),
        P(None, None, "tensor"),
        P(None, None, "tensor"),
        P(None, "tensor", None),
        P("dp", None),
    )
    return jax.shard_map(
        shards,
        mesh=mesh,
        in_specs=placed,
        out_specs=(
            P("dp", None),
            P("dp", None),
            P(None, "dp"),
            P(None, "dp"),
            P(None, "dp", "tensor"),
            P(None, "dp", "tensor"),
            P(None, "dp", "tensor"),
            P(None, "tensor", "dp"),
            P(None, "dp", "tensor"),
            P(None, "dp", "tensor"),
            P(None, "tensor", "dp"),
        ),
        check_vma=False,
    )
```

profile of v0, /device:TPU:0, one launch (start us, length us, event | category | flops | bytes accessed | tf_op | source)
XLA Modules:
  0.0 1885.0 jit_solution(11726850413629536480)
XLA Ops:
  38.5 14.9 collective-permute-done.5
  53.4 4.6 fusion.10
  63.8 4.4 convolution_convert_fusion.15
  72.2 64.6 %all-reduce.13.cloned.1.call-done = f32[512,1536]{1,0:T(8,128)} async-done(((f32[512,1536]{1,0:T(8,128)}), f32[512,1536]{1,0:T(8,128)}) %all-reduce.13.cloned.1.call-update) | async-done | bytes 3145744 | tf_op jit(solution)/shard_map/psum | solution.py:131
  140.5 4.5 fusion.38
  155.3 66.3 %all-reduce.15.cloned.1.call-done = f32[512,1536]{1,0:T(8,128)} async-done(((f32[512,1536]{1,0:T(8,128)}), f32[512,1536]{1,0:T(8,128)}) %all-reduce.15.cloned.1.call-update) | async-done | bytes 3145744 | tf_op jit(solution)/shard_map/psum | solution.py:138
  238.2 22.7 %collective-permute-done.11 = bf16[512,192]{0,1:T(8,128)(2,1)S(1)} collective-permute-done((bf16[512,192]{0,1:T(8,128)(2,1)S(1)}, bf16[512,192]{0,1:T(8,128)(2,1)S(1)}, u32[]{:S(2)}, u32[]{:S(2)}) %collective-permute-start.11) | collective-permute-done | bytes 196640 | tf_op jit(solution)/shard_map/ppermute | solution.py:16
  269.7 4.4 convolution_convert_fusion.14
  279.3 64.6 %all-reduce.17.cloned.1.call-done = f32[512,1536]{1,0:T(8,128)} async-done(((f32[512,1536]{1,0:T(8,128)}), f32[512,1536]{1,0:T(8,128)}) %all-reduce.17.cloned.1.call-update) | async-done | bytes 3145744 | tf_op jit(solution)/shard_map/psum | solution.py:131
  347.7 5.6 fusion.23
  365.1 68.7 %all-reduce.19.cloned.1.call-done = f32[512,1536]{1,0:T(8,128)} async-done(((f32[512,1536]{1,0:T(8,128)}), f32[512,1536]{1,0:T(8,128)}) %all-reduce.19.cloned.1.call-update) | async-done | bytes 3145744 | tf_op jit(solution)/shard_map/psum | solution.py:193
  433.7 4.3 multiply_reduce_fusion
  444.3 9.5 convolution_bitcast_fusion.1
  453.8 8.2 fusion.188
  462.0 25.3 %fusion.63 = f32[2048,2,96]{0,2,1:T(8,128)} fusion(bf16[512,2,2,96]{0,3,2,1:T(8,128)(2,1)} %bitcast.491, f32[2,2048,512,2]{2,1,3,0:T(8,128)} %fusion.188, f32[2,2048,512,2]{2,1,3,0:T(8,128)} %copy-done.12, f32[2,2,512]{2,1,0:T(2,128)} %copy-done.94, pred[512,2048]{0,1:T(8,128)(4,1)} %copy-done.25), kind=kOutput, calls=%fused_computation.113 | convolution fusion | flops 851447808 | bytes 36577280 | tf_op jit(solution)/shard_map/kgqt,qkgd->tkd/dot_general | solution.py:83
  487.3 25.1 %fusion.41 = f32[2,96,2,512]{3,1,2,0:T(8,128)} fusion(f32[2,2048,512,2]{2,1,3,0:T(8,128)} %fusion.188, f32[2,2048,512,2]{2,1,3,0:T(8,128)} %copy-done.12, f32[2,2,512]{2,1,0:T(2,128)} %copy-done.94, pred[512,2048]{0,1:T(8,128)(4,1)} %copy-done.25, bf16[512,2,96]{0,2,1:T(8,128)(2,1)} %bitcast.530, bf16[512,2,96]{0,2,1:T(8,128)(2,1)} %bitcast.528, ...), kind=kOutput, calls=%fused_computation.87 | convolution fusion | flops 854593536 | bytes 36184064 | tf_op jit(solution)/shard_map/kgqt,tkd->qkgd/dot_general | solution.py:80
  514.0 4.3 collective-permute-start.15
  525.8 19.0 %collective-permute-done.12 = f32[512,192]{0,1:T(8,128)S(1)} collective-permute-done((f32[512,192]{0,1:T(8,128)S(1)}, f32[512,192]{0,1:T(8,128)S(1)}, u32[]{:S(2)}, u32[]{:S(2)}) %collective-permute-start.12) | collective-permute-done | bytes 393248 | tf_op jit(solution)/shard_map/ppermute | solution.py:16
  547.4 5.8 collective-permute-done.13
  553.2 8.4 collective-permute-done.14
  562.7 6.1 collective-permute-done.17
  571.9 86.6 %all-reduce.21.cloned.1.call-done = f32[512,1536]{1,0:T(8,128)} async-done(((f32[512,1536]{1,0:T(8,128)}), f32[512,1536]{1,0:T(8,128)}) %all-reduce.21.cloned.1.call-update) | async-done | bytes 3145744 | tf_op jit(solution)/shard_map/psum | solution.py:229
  658.6 4.3 multiply_reduce_fusion.2
  666.2 6.6 multiply_convert_fusion.4
  678.5 5.7 fusion.20
  684.1 63.0 %all-reduce.23.cloned.1.call-done = f32[512,1536]{1,0:T(8,128)} async-done(((f32[512,1536]{1,0:T(8,128)}), f32[512,1536]{1,0:T(8,128)}) %all-reduce.23.cloned.1.call-update) | async-done | bytes 3145744 | tf_op jit(solution)/shard_map/psum | solution.py:193
  754.7 9.7 convolution_bitcast_fusion
  764.4 8.1 fusion.189
  772.5 24.6 %fusion.62 = f32[2048,2,96]{0,2,1:T(8,128)} fusion(bf16[512,2,2,96]{0,3,2,1:T(8,128)(2,1)S(1)} %bitcast.489, f32[2,2048,512,2]{2,1,3,0:T(8,128)} %fusion.189, f32[2,2048,512,2]{2,1,3,0:T(8,128)} %copy-done.11, f32[2,2,512]{2,1,0:T(2,128)S(1)} %copy-done.93, pred[512,2048]{0,1:T(8,128)(4,1)S(1)} %copy-done.28), kind=kOutput, calls=%fused_computation.112 | convolution fusion | flops 851447808 | bytes 36577280 | tf_op jit(solution)/shard_map/kgqt,qkgd->tkd/dot_general | solution.py:83
  797.2 23.6 %fusion.44 = f32[2,96,2,512]{3,1,2,0:T(8,128)S(1)} fusion(f32[2,2048,512,2]{2,1,3,0:T(8,128)} %fusion.189, f32[2,2048,512,2]{2,1,3,0:T(8,128)} %copy-done.11, f32[2,2,512]{2,1,0:T(2,128)S(1)} %copy-done.93, pred[512,2048]{0,1:T(8,128)(4,1)S(1)} %copy-done.28, bf16[512,2,96]{0,2,1:T(8,128)(2,1)} %bitcast.14, bf16[512,2,96]{0,2,1:T(8,128)(2,1)} %bitcast.13, ...), kind=kOutput, calls=%fused_computation.90 | convolution fusion | flops 854593536 | bytes 36184064 | tf_op jit(solution)/shard_map/kgqt,tkd->qkgd/dot_general | solution.py:80
  822.6 4.3 collective-permute-start.21
  834.4 19.0 %collective-permute-done.18 = f32[512,192]{0,1:T(8,128)S(1)} collective-permute-done((f32[512,192]{0,1:T(8,128)S(1)}, f32[512,192]{0,1:T(8,128)S(1)}, u32[]{:S(2)}, u32[]{:S(2)}) %collective-permute-start.18) | collective-permute-done | bytes 393248 | tf_op jit(solution)/shard_map/ppermute | solution.py:16
  855.9 5.9 collective-permute-done.19
  861.8 8.4 collective-permute-done.20
  871.3 6.1 collective-permute-done.23
  887.9 4.9 copy.91
  892.7 4.5 reshape.440
  913.4 105.2 %all-reduce.25.cloned.1.call-done = (f32[512,1536]{1,0:T(8,128)}, f32[512,1536]{1,0:T(8,128)}) async-done(((f32[512,1536]{1,0:T(8,128)}, f32[512,1536]{1,0:T(8,128)}), (f32[512,1536]{1,0:T(8,128)}, f32[512,1536]{1,0:T(8,128)})) %all-reduce.25.cloned.1.call-update) | async-done | bytes 6291472 | tf_op jit(solution)/shard_map/psum | solution.py:138
  1037.8 16.4 copy.64
  1058.7 6.8 copy.63
  1086.7 63.9 %reduce-scatter.28.cloned.1.call-done = bf16[192,384]{1,0:T(8,128)(2,1)} async-done(((bf16[1536,384]{1,0:T(8,128)(2,1)}), bf16[192,384]{1,0:T(8,128)(2,1)}) %reduce-scatter.28.cloned.1.call-update) | async-done | bytes 147472
  1152.8 64.8 %reduce-scatter.26.cloned.1.call-done = bf16[192,384]{1,0:T(8,128)(2,1)} async-done(((bf16[1536,384]{1,0:T(8,128)(2,1)}), bf16[192,384]{1,0:T(8,128)(2,1)}) %reduce-scatter.26.cloned.1.call-update) | async-done | bytes 147472
  1219.7 5.2 add.306
  1227.4 54.4 %reduce-scatter.22.cloned.1.call-done = bf16[192,2]{1,0:T(8,128)(2,1)} async-done(((bf16[1536,2]{1,0:T(8,128)(2,1)}), bf16[192,2]{1,0:T(8,128)(2,1)}) %reduce-scatter.22.cloned.1.call-update) | async-done | bytes 784
  1283.3 69.9 %reduce-scatter.16.cloned.1.call-done = bf16[2,192,384]{2,1,0:T(8,128)(2,1)} async-done(((bf16[2,1536,384]{2,1,0:T(8,128)(2,1)}), bf16[2,192,384]{2,1,0:T(8,128)(2,1)}) %reduce-scatter.16.cloned.1.call-update) | async-done | bytes 294928 | tf_op jit(solution)/shard_map/reduce_scatter | solution.py:327
  1355.0 278.8 %all-reduce.27.cloned.1.call-done = (bf16[2,384,1536]{1,0,2:T(2,128)(2,1)}, bf16[2,1024,1536]{1,0,2:T(2,128)(2,1)}) async-done(((bf16[2,384,1536]{1,0,2:T(2,128)(2,1)}, bf16[2,1024,1536]{1,0,2:T(2,128)(2,1)}), (bf16[2,384,1536]{1,0,2:T(2,128)(2,1)}, bf16[2,1024,1536]{1,0,2:T(2,128)(2,1)})) %all-reduce.27.cloned.1.call-update) | async-done | bytes 8650768
  1639.1 115.5 %reduce-scatter.20.cloned.1.call-done = bf16[2,192,1024]{2,1,0:T(8,128)(2,1)} async-done(((bf16[2,1536,1024]{2,1,0:T(8,128)(2,1)}), bf16[2,192,1024]{2,1,0:T(8,128)(2,1)}) %reduce-scatter.20.cloned.1.call-update) | async-done | bytes 786448 | tf_op jit(solution)/shard_map/reduce_scatter | solution.py:342
  1757.1 118.5 %reduce-scatter.18.cloned.1.call-done = bf16[2,192,1024]{2,1,0:T(8,128)(2,1)} async-done(((bf16[2,1536,1024]{2,1,0:T(8,128)(2,1)}), bf16[2,192,1024]{2,1,0:T(8,128)(2,1)}) %reduce-scatter.18.cloned.1.call-update) | async-done | bytes 786448 | tf_op jit(solution)/shard_map/reduce_scatter | solution.py:339
  (479 shorter events, 242.2 us)
Async XLA Ops:
  7.2 129.6 %all-reduce.13.cloned.1.call-start = ((), (), s32[]{:S(2)}) async-start(), calls=%async_computation.7 | async-start | bytes 6291456 | tf_op jit(solution)/shard_map/psum | solution.py:131
  16.8 19.0 %collective-permute-start.3 = (bf16[512,192]{0,1:T(8,128)(2,1)}, bf16[512,192]{0,1:T(8,128)(2,1)}, u32[]{:S(2)}, u32[]{:S(2)}) collective-permute-start(bf16[512,192]{0,1:T(8,128)(2,1)} %bitcast.11), channel_id=1, source_target_pairs={{28,0},{0,4},{4,8},{8,12},{12,16},{16,20},{20,24},{24,28},{29,1},{... | collective-permute-start | bytes 589832 | tf_op jit(solution)/shard_map/ppermute | solution.py:16
  19.7 18.7 collective-permute-start.4
  21.3 32.1 %collective-permute-start.5 = (bf16[512,192]{0,1:T(8,128)(2,1)}, bf16[512,192]{0,1:T(8,128)(2,1)}, u32[]{:S(2)}, u32[]{:S(2)}) collective-permute-start(bf16[512,192]{0,1:T(8,128)(2,1)} %bitcast.11), channel_id=1, source_target_pairs={{20,0},{24,4},{28,8},{0,12},{4,16},{8,20},{12,24},{16,28},{21,1},{... | collective-permute-start | bytes 589832 | tf_op jit(solution)/shard_map/ppermute | solution.py:16
  24.6 37.1 %collective-permute-start = (bf16[512,192]{0,1:T(8,128)(2,1)S(1)}, bf16[512,192]{0,1:T(8,128)(2,1)S(1)}, u32[]{:S(2)}, u32[]{:S(2)}) collective-permute-start(bf16[512,192]{0,1:T(8,128)(2,1)S(1)} %convolution_convert_fusion.19), channel_id=1, source_target_pairs={{28,0},{0,4},{4,8},{8,12},{12,16},{16,20},{20,24},{24,28},{29,1},{... | collective-permute-start | bytes 589832 | tf_op jit(solution)/shard_map/ppermute | solution.py:16
  26.1 35.6 %collective-permute-start.1 = (bf16[512,192]{0,1:T(8,128)(2,1)S(1)}, bf16[512,192]{0,1:T(8,128)(2,1)}, u32[]{:S(2)}, u32[]{:S(2)}) collective-permute-start(bf16[512,192]{0,1:T(8,128)(2,1)S(1)} %convolution_convert_fusion.19), channel_id=1, source_target_pairs={{24,0},{28,4},{0,8},{4,12},{8,16},{12,20},{16,24},{20,28},{25,1},{... | collective-permute-start | bytes 589832 | tf_op jit(solution)/shard_map/ppermute | solution.py:16
  35.6 27.4 %copy-start.25 = (pred[512,2048]{0,1:T(8,128)(4,1)}, pred[512,2048]{0,1:T(8,128)(4,1)S(1)}, u32[]{:S(2)}) copy-start(pred[512,2048]{0,1:T(8,128)(4,1)S(1)} %compare_and_fusion) | copy-start | bytes 3145732
  35.8 25.9 %collective-permute-start.2 = (bf16[512,192]{0,1:T(8,128)(2,1)S(1)}, bf16[512,192]{0,1:T(8,128)(2,1)S(1)}, u32[]{:S(2)}, u32[]{:S(2)}) collective-permute-start(bf16[512,192]{0,1:T(8,128)(2,1)S(1)} %convolution_convert_fusion.19), channel_id=1, source_target_pairs={{20,0},{24,4},{28,8},{0,12},{4,16},{8,20},{12,24},{16,28},{21,1},{... | collective-permute-start | bytes 589832 | tf_op jit(solution)/shard_map/ppermute | solution.py:16
  70.9 150.6 %all-reduce.15.cloned.1.call-start = ((), (), s32[]{:S(2)}) async-start(), calls=%async_computation.8 | async-start | bytes 6291456 | tf_op jit(solution)/shard_map/psum | solution.py:138
  152.9 191.1 %all-reduce.17.cloned.1.call-start = ((), (), s32[]{:S(2)}) async-start(), calls=%async_computation.9 | async-start | bytes 6291456 | tf_op jit(solution)/shard_map/psum | solution.py:131
  226.2 34.7 %copy-start.71 = (bf16[512,2,96]{0,2,1:T(8,128)(2,1)}, bf16[512,2,96]{0,2,1:T(8,128)(2,1)S(1)}, u32[]{:S(2)}) copy-start(bf16[512,2,96]{0,2,1:T(8,128)(2,1)S(1)} %fusion.129) | copy-start | bytes 589828
  226.2 10.7 collective-permute-start.9
  227.8 10.5 collective-permute-start.10
  229.2 31.6 %collective-permute-start.11 = (bf16[512,192]{0,1:T(8,128)(2,1)S(1)}, bf16[512,192]{0,1:T(8,128)(2,1)S(1)}, u32[]{:S(2)}, u32[]{:S(2)}) collective-permute-start(bf16[512,192]{0,1:T(8,128)(2,1)S(1)} %bitcast.506), channel_id=1, source_target_pairs={{20,0},{24,4},{28,8},{0,12},{4,16},{8,20},{12,24},{16,28},{21,1},{... | collective-permute-start | bytes 589832 | tf_op jit(solution)/shard_map/ppermute | solution.py:16
  232.3 35.3 %collective-permute-start.6 = (bf16[512,192]{0,1:T(8,128)(2,1)S(1)}, bf16[512,192]{0,1:T(8,128)(2,1)S(1)}, u32[]{:S(2)}, u32[]{:S(2)}) collective-permute-start(bf16[512,192]{0,1:T(8,128)(2,1)S(1)} %convolution_convert_fusion.18), channel_id=1, source_target_pairs={{28,0},{0,4},{4,8},{8,12},{12,16},{16,20},{20,24},{24,28},{29,1},{... | collective-permute-start | bytes 589832 | tf_op jit(solution)/shard_map/ppermute | solution.py:16
  233.8 33.8 %collective-permute-start.7 = (bf16[512,192]{0,1:T(8,128)(2,1)S(1)}, bf16[512,192]{0,1:T(8,128)(2,1)S(1)}, u32[]{:S(2)}, u32[]{:S(2)}) collective-permute-start(bf16[512,192]{0,1:T(8,128)(2,1)S(1)} %convolution_convert_fusion.18), channel_id=1, source_target_pairs={{24,0},{28,4},{0,8},{4,12},{8,16},{12,20},{16,24},{20,28},{25,1},{... | collective-permute-start | bytes 589832 | tf_op jit(solution)/shard_map/ppermute | solution.py:16
  235.5 28.4 %copy-start.70 = (bf16[512,4,96]{0,2,1:T(8,128)(2,1)}, bf16[512,4,96]{0,2,1:T(8,128)(2,1)S(1)}, u32[]{:S(2)}) copy-start(bf16[512,4,96]{0,2,1:T(8,128)(2,1)S(1)} %fusion.99) | copy-start | bytes 1179652
  236.9 30.8 %collective-permute-start.8 = (bf16[512,192]{0,1:T(8,128)(2,1)S(1)}, bf16[512,192]{0,1:T(8,128)(2,1)S(1)}, u32[]{:S(2)}, u32[]{:S(2)}) collective-permute-start(bf16[512,192]{0,1:T(8,128)(2,1)S(1)} %convolution_convert_fusion.18), channel_id=1, source_target_pairs={{20,0},{24,4},{28,8},{0,12},{4,16},{8,20},{12,24},{16,28},{21,1},{... | collective-permute-start | bytes 589832 | tf_op jit(solution)/shard_map/ppermute | solution.py:16
  278.8 154.9 %all-reduce.19.cloned.1.call-start = ((), (), s32[]{:S(2)}) async-start(), calls=%async_computation.10 | async-start | bytes 6291456 | tf_op jit(solution)/shard_map/psum | solution.py:193
  365.0 293.5 %all-reduce.21.cloned.1.call-start = ((), (), s32[]{:S(2)}) async-start(), calls=%async_computation.11 | async-start | bytes 6291456 | tf_op jit(solution)/shard_map/psum | solution.py:229
  514.0 48.6 %collective-permute-start.15 = (f32[512,192]{0,1:T(8,128)S(1)}, f32[512,192]{0,1:T(8,128)S(1)}, u32[]{:S(2)}, u32[]{:S(2)}) collective-permute-start(f32[512,192]{0,1:T(8,128)S(1)} %bitcast.497), channel_id=1, source_target_pairs={{4,0},{8,4},{12,8},{16,12},{20,16},{24,20},{28,24},{0,28},{5,1},{9... | collective-permute-start | bytes 1179656 | tf_op jit(solution)/shard_map/ppermute | solution.py:16
  518.3 44.4 %collective-permute-start.16 = (f32[512,192]{0,1:T(8,128)S(1)}, f32[512,192]{0,1:T(8,128)S(1)}, u32[]{:S(2)}, u32[]{:S(2)}) collective-permute-start(f32[512,192]{0,1:T(8,128)S(1)} %bitcast.495), channel_id=1, source_target_pairs={{8,0},{12,4},{16,8},{20,12},{24,16},{28,20},{0,24},{4,28},{9,1},{1... | collective-permute-start | bytes 1179656 | tf_op jit(solution)/shard_map/ppermute | solution.py:16
  519.0 25.7 %collective-permute-start.12 = (f32[512,192]{0,1:T(8,128)S(1)}, f32[512,192]{0,1:T(8,128)S(1)}, u32[]{:S(2)}, u32[]{:S(2)}) collective-permute-start(f32[512,192]{0,1:T(8,128)S(1)} %bitcast.502), channel_id=1, source_target_pairs={{4,0},{8,4},{12,8},{16,12},{20,16},{24,20},{28,24},{0,28},{5,1},{9... | collective-permute-start | bytes 1179656 | tf_op jit(solution)/shard_map/ppermute | solution.py:16
  519.6 33.6 %collective-permute-start.13 = (f32[512,192]{0,1:T(8,128)S(1)}, f32[512,192]{0,1:T(8,128)S(1)}, u32[]{:S(2)}, u32[]{:S(2)}) collective-permute-start(f32[512,192]{0,1:T(8,128)S(1)} %bitcast.500), channel_id=1, source_target_pairs={{8,0},{12,4},{16,8},{20,12},{24,16},{28,20},{0,24},{4,28},{9,1},{1... | collective-permute-start | bytes 1179656 | tf_op jit(solution)/shard_map/ppermute | solution.py:16
  520.2 41.4 %collective-permute-start.14 = (f32[512,192]{0,1:T(8,128)S(1)}, f32[512,192]{0,1:T(8,128)S(1)}, u32[]{:S(2)}, u32[]{:S(2)}) collective-permute-start(f32[512,192]{0,1:T(8,128)S(1)} %bitcast.498), channel_id=1, source_target_pairs={{12,0},{16,4},{20,8},{24,12},{28,16},{0,20},{4,24},{8,28},{13,1},{... | collective-permute-start | bytes 1179656 | tf_op jit(solution)/shard_map/ppermute | solution.py:16
  525.8 36.2 %copy-start.38 = (bf16[2,1536,192]{1,2,0:T(8,128)(2,1)S(1)}, bf16[2,1536,192]{1,2,0:T(8,128)(2,1)}, u32[]{:S(2)}) copy-start(bf16[2,1536,192]{1,2,0:T(8,128)(2,1)} %param.17) | copy-start | bytes 3538948
  544.8 24.0 %collective-permute-start.17 = (f32[512,192]{0,1:T(8,128)S(1)}, f32[512,192]{0,1:T(8,128)S(1)}, u32[]{:S(2)}, u32[]{:S(2)}) collective-permute-start(f32[512,192]{0,1:T(8,128)S(1)} %bitcast.493), channel_id=1, source_target_pairs={{12,0},{16,4},{20,8},{24,12},{28,16},{0,20},{4,24},{8,28},{13,1},{... | collective-permute-start | bytes 1179656 | tf_op jit(solution)/shard_map/ppermute | solution.py:16
  571.9 175.2 %all-reduce.23.cloned.1.call-start = ((), (), s32[]{:S(2)}) async-start(), calls=%async_computation.12 | async-start | bytes 6291456 | tf_op jit(solution)/shard_map/psum | solution.py:193
  678.4 340.1 %all-reduce.25.cloned.1.call-start = ((), (), s32[]{:S(2)}) async-start(), calls=%async_computation.20 | async-start | bytes 12582912 | tf_op jit(solution)/shard_map/psum | solution.py:138
  678.5 68.7 %copy-start.82 = (f32[512]{0:T(512)S(1)}, f32[512]{0:T(512)}, u32[]{:S(2)}) copy-start(f32[512]{0:T(512)} %copy-done.81) | copy-start | bytes 6148
  822.6 48.6 %collective-permute-start.21 = (f32[512,192]{0,1:T(8,128)S(1)}, f32[512,192]{0,1:T(8,128)S(1)}, u32[]{:S(2)}, u32[]{:S(2)}) collective-permute-start(f32[512,192]{0,1:T(8,128)S(1)} %bitcast.496), channel_id=1, source_target_pairs={{4,0},{8,4},{12,8},{16,12},{20,16},{24,20},{28,24},{0,28},{5,1},{9... | collective-permute-start | bytes 1179656 | tf_op jit(solution)/shard_map/ppermute | solution.py:16
  826.9 44.4 %collective-permute-start.22 = (f32[512,192]{0,1:T(8,128)S(1)}, f32[512,192]{0,1:T(8,128)S(1)}, u32[]{:S(2)}, u32[]{:S(2)}) collective-permute-start(f32[512,192]{0,1:T(8,128)S(1)} %bitcast.494), channel_id=1, source_target_pairs={{8,0},{12,4},{16,8},{20,12},{24,16},{28,20},{0,24},{4,28},{9,1},{1... | collective-permute-start | bytes 1179656 | tf_op jit(solution)/shard_map/ppermute | solution.py:16
  827.6 25.7 %collective-permute-start.18 = (f32[512,192]{0,1:T(8,128)S(1)}, f32[512,192]{0,1:T(8,128)S(1)}, u32[]{:S(2)}, u32[]{:S(2)}) collective-permute-start(f32[512,192]{0,1:T(8,128)S(1)} %bitcast.503), channel_id=1, source_target_pairs={{4,0},{8,4},{12,8},{16,12},{20,16},{24,20},{28,24},{0,28},{5,1},{9... | collective-permute-start | bytes 1179656 | tf_op jit(solution)/shard_map/ppermute | solution.py:16
  828.2 33.6 %collective-permute-start.19 = (f32[512,192]{0,1:T(8,128)S(1)}, f32[512,192]{0,1:T(8,128)S(1)}, u32[]{:S(2)}, u32[]{:S(2)}) collective-permute-start(f32[512,192]{0,1:T(8,128)S(1)} %bitcast.501), channel_id=1, source_target_pairs={{8,0},{12,4},{16,8},{20,12},{24,16},{28,20},{0,24},{4,28},{9,1},{1... | collective-permute-start | bytes 1179656 | tf_op jit(solution)/shard_map/ppermute | solution.py:16
  828.8 41.4 %collective-permute-start.20 = (f32[512,192]{0,1:T(8,128)S(1)}, f32[512,192]{0,1:T(8,128)S(1)}, u32[]{:S(2)}, u32[]{:S(2)}) collective-permute-start(f32[512,192]{0,1:T(8,128)S(1)} %bitcast.499), channel_id=1, source_target_pairs={{12,0},{16,4},{20,8},{24,12},{28,16},{0,20},{4,24},{8,28},{13,1},{... | collective-permute-start | bytes 1179656 | tf_op jit(solution)/shard_map/ppermute | solution.py:16
  834.4 36.2 %copy-start.39 = (bf16[2,1536,192]{1,2,0:T(8,128)(2,1)S(1)}, bf16[2,1536,192]{1,2,0:T(8,128)(2,1)}, u32[]{:S(2)}) copy-start(bf16[2,1536,192]{1,2,0:T(8,128)(2,1)} %param.17) | copy-start | bytes 3538948
  853.4 24.0 %collective-permute-start.23 = (f32[512,192]{0,1:T(8,128)S(1)}, f32[512,192]{0,1:T(8,128)S(1)}, u32[]{:S(2)}, u32[]{:S(2)}) collective-permute-start(f32[512,192]{0,1:T(8,128)S(1)} %bitcast.492), channel_id=1, source_target_pairs={{12,0},{16,4},{20,8},{24,12},{28,16},{0,20},{4,24},{8,28},{13,1},{... | collective-permute-start | bytes 1179656 | tf_op jit(solution)/shard_map/ppermute | solution.py:16
  880.5 204.7 %reduce-scatter.24.cloned.1.call-start = ((), (), s32[]{:S(2)}) async-start(), calls=%async_computation.17 | async-start | bytes 442368
  884.2 266.5 %reduce-scatter.28.cloned.1.call-start = ((), (), s32[]{:S(2)}) async-start(), calls=%async_computation.19 | async-start | bytes 1327104
  897.3 320.3 %reduce-scatter.26.cloned.1.call-start = ((), (), s32[]{:S(2)}) async-start(), calls=%async_computation.18 | async-start | bytes 1327104
  905.8 376.0 %reduce-scatter.22.cloned.1.call-start = ((), (), s32[]{:S(2)}) async-start(), calls=%async_computation.16 | async-start | bytes 442368
  907.7 110.8 %copy-start.3 = (f32[512,1536]{1,0:T(8,128)S(1)}, f32[512,1536]{1,0:T(8,128)}, u32[]{:S(2)}) copy-start(f32[512,1536]{1,0:T(8,128)} %param.12) | copy-start | bytes 9437188
  907.7 110.8 %copy-start.73 = (f32[1536]{0:T(1024)S(1)}, f32[1536]{0:T(1024)}, u32[]{:S(2)}) copy-start(f32[1536]{0:T(1024)} %copy-done.72) | copy-start | bytes 18436
  907.7 110.8 %copy-start.80 = (f32[512]{0:T(512)S(1)}, f32[512]{0:T(512)}, u32[]{:S(2)}) copy-start(f32[512]{0:T(512)} %copy-done.79) | copy-start | bytes 6148
  1022.2 331.0 %reduce-scatter.16.cloned.1.call-start = ((), (), s32[]{:S(2)}) async-start(), calls=%async_computation.13 | async-start | bytes 2654208 | tf_op jit(solution)/shard_map/reduce_scatter | solution.py:327
  1025.6 608.2 %all-reduce.27.cloned.1.call-start = ((), (), s32[]{:S(2)}) async-start(), calls=%async_computation.21 | async-start | bytes 17301504
  1065.5 689.1 %reduce-scatter.20.cloned.1.call-start = ((), (), s32[]{:S(2)}) async-start(), calls=%async_computation.15 | async-start | bytes 7077888 | tf_op jit(solution)/shard_map/reduce_scatter | solution.py:342
  1074.3 801.3 %reduce-scatter.18.cloned.1.call-start = ((), (), s32[]{:S(2)}) async-start(), calls=%async_computation.14 | async-start | bytes 7077888 | tf_op jit(solution)/shard_map/reduce_scatter | solution.py:339
  (117 other events, 633.8 us)
Sparse Core Ops, SparseCore 0:
  71.1 65.7 all-reduce.12
  153.0 68.5 all-reduce.14
  278.9 64.9 all-reduce.16
  365.1 68.5 all-reduce.18
  572.0 86.5 all-reduce.20
  678.5 68.5 all-reduce.22
  880.6 137.8 all-reduce.24
  1022.4 61.5 reduce-scatter.23
  1087.4 63.2 reduce-scatter.27
  1154.5 63.0 reduce-scatter.25
  1221.4 60.3 reduce-scatter.21
  1285.1 68.0 reduce-scatter.15
  1357.2 276.5 all-reduce.26
  1637.7 116.9 reduce-scatter.19
  1758.5 117.0 reduce-scatter.17
where the time goes:
time: 1890 us; the launch traced here: 1880 us
  waiting for transfers between devices  1400 us (74%)
  matrix products  249 us (13%)
  other arithmetic  89 us (5%)
  local copies, waits for them, and re-layouts  81.4 us (4%)
  starting transfers between devices  45.7 us (2%)
    unnamed x20, waiting for transfers between devices  462 us
    psum x2, waiting for transfers between devices, forward_layer(): result = middle + lax.psum(unit_part, 'tensor')  171 us
    psum x2, waiting for transfers between devices, backward_layer(): mlp_norm_grad = lax.psum(unit_back, 'tensor')  132 us
    psum x2, waiting for transfers between devices, forward_layer(): middle = residual_stream + lax.psum(head_part, 'tensor')  129 us
    reduce_scatter x1, waiting for transfers between devices, shards(): lax.psum_scatter(stacked[6].astype(jnp.bfloat16), 'dp', scatter_dimension...  119 us
    ppermute x24, waiting for transfers between devices, passed_along(): return lax.ppermute(block, axis, route)  118 us
    reduce_scatter x1, waiting for transfers between devices, shards(): lax.psum_scatter(stacked[7].astype(jnp.bfloat16), 'dp', scatter_dimension...  116 us
    psum x1, waiting for transfers between devices, backward_layer(): attn_norm_grad = lax.psum(head_back, 'tensor')  86.6 us
  transfers between devices with their start and end apart: 39, of which 25 were waited for; matrix products, arithmetic and copies ran while one was open for 9% of the time, Pallas kernels for 0%

commit v1 on v0

--- a/solution.py
+++ b/solution.py
@@ -135,7 +135,12 @@
     up_values = jnp.dot(normed_mlp, up_w, preferred_element_type=jnp.float32)
     activated = (jax.nn.silu(gate_pre) * up_values).astype(jnp.bfloat16)
     unit_part = jnp.dot(activated, down_w, preferred_element_type=jnp.float32)
-    result = middle + lax.psum(unit_part, "tensor")
+
+    def move_goods(x_in):
+        block_now = lax.all_gather(x_in, axis_name="tensor")
+        return jnp.sum(block_now, 0)
+
+    result = middle + move_goods(unit_part)
     record = (
         residual_stream,
         inv_attn,

time: 1890 us -> 1960 us (1.037)
  waiting for transfers between devices: 1400 us -> 1440 us
    psum x2 -> x0, waiting for transfers between devices: 171 us -> none  [forward_layer(): result = middle + lax.psum(unit_part, 'tensor')]
    all_gather x0 -> x2, waiting for transfers between devices: none -> 159 us  [move_goods(): block_now = lax.all_gather(x_in, axis_name='tensor')]
    psum x1 -> x2, waiting for transfers between devices: 86.6 us -> 164 us  [backward_layer(): attn_norm_grad = lax.psum(head_back, 'tensor')]
    unnamed x20 -> x21, waiting for transfers between devices: 462 us -> 436 us
    unnamed x269 -> x253, local copies, waits for them, and re-layouts: 43.1 us -> 45.5 us
  transfers between devices with their start and end apart: 39 -> 40, of which waited for: 25 -> 26; matrix products, arithmetic and copies ran while one was open for 9% -> 9% of each run, Pallas kernels for 0% -> 0%
where the time goes in v1:
time: 1960 us; the launch traced here: 1950 us
  waiting for transfers between devices  1440 us (73%)
  matrix products  251 us (13%)
  other arithmetic  107 us (5%)
  local copies, waits for them, and re-layouts  85.2 us (4%)
  starting transfers between devices  46.2 us (2%)
    unnamed x21, waiting for transfers between devices  436 us
    psum x2, waiting for transfers between devices, backward_layer(): attn_norm_grad = lax.psum(head_back, 'tensor')  164 us
    all_gather x2, waiting for transfers between devices, move_goods(): block_now = lax.all_gather(x_in, axis_name='tensor')  159 us
    psum x2, waiting for transfers between devices, backward_layer(): mlp_norm_grad = lax.psum(unit_back, 'tensor')  132 us
    psum x2, waiting for transfers between devices, forward_layer(): middle = residual_stream + lax.psum(head_part, 'tensor')  129 us
    reduce_scatter x1, waiting for transfers between devices, shards(): lax.psum_scatter(stacked[6].astype(jnp.bfloat16), 'dp', scatter_dimension...  119 us
    ppermute x24, waiting for transfers between devices, passed_along(): return lax.ppermute(block, axis, route)  118 us
    reduce_scatter x1, waiting for transfers between devices, shards(): lax.psum_scatter(stacked[7].astype(jnp.bfloat16), 'dp', scatter_dimension...  115 us
  transfers between devices with their start and end apart: 40, of which 26 were waited for; matrix products, arithmetic and copies ran while one was open for 9% of the time, Pallas kernels for 0%

profile of v1, /device:TPU:0, one launch (start us, length us, event | category | flops | bytes accessed | tf_op | source)
XLA Modules:
  0.0 1946.8 jit_solution(11635481319433784794)
XLA Ops:
  38.5 14.9 collective-permute-done.5
  53.4 4.6 fusion.10
  72.3 64.6 %all-reduce.11.cloned.1.call-done = f32[512,1536]{1,0:T(8,128)} async-done(((f32[512,1536]{1,0:T(8,128)}), f32[512,1536]{1,0:T(8,128)}) %all-reduce.11.cloned.1.call-update) | async-done | bytes 3145744 | tf_op jit(solution)/shard_map/psum | solution.py:131
  155.4 79.9 %all-gather.5.cloned.1.call-done = f32[2048,1536]{1,0:T(8,128)} async-done(((f32[512,1536]{1,0:T(8,128)}), f32[2048,1536]{1,0:T(8,128)}) %all-gather.5.cloned.1.call-update) | async-done | bytes 12582928 | tf_op jit(solution)/shard_map/all_gather | solution.py:140
  235.4 8.0 reduce_sum.195
  260.3 22.9 %collective-permute-done.11 = bf16[512,192]{0,1:T(8,128)(2,1)S(1)} collective-permute-done((bf16[512,192]{0,1:T(8,128)(2,1)S(1)}, bf16[512,192]{0,1:T(8,128)(2,1)S(1)}, u32[]{:S(2)}, u32[]{:S(2)}) %collective-permute-start.11) | collective-permute-done | bytes 196640 | tf_op jit(solution)/shard_map/ppermute | solution.py:16
  301.4 64.5 %all-reduce.13.cloned.1.call-done = f32[512,1536]{1,0:T(8,128)} async-done(((f32[512,1536]{1,0:T(8,128)}), f32[512,1536]{1,0:T(8,128)}) %all-reduce.13.cloned.1.call-update) | async-done | bytes 3145744 | tf_op jit(solution)/shard_map/psum | solution.py:131
  369.7 5.6 fusion.23
  387.0 5.7 fusion.20
  392.8 62.9 %all-reduce.15.cloned.1.call-done = f32[512,1536]{1,0:T(8,128)} async-done(((f32[512,1536]{1,0:T(8,128)}), f32[512,1536]{1,0:T(8,128)}) %all-reduce.15.cloned.1.call-update) | async-done | bytes 3145744 | tf_op jit(solution)/shard_map/psum | solution.py:198
  460.5 78.8 %all-gather.7.cloned.1.call-done = f32[2048,1536]{1,0:T(8,128)} async-done(((f32[512,1536]{1,0:T(8,128)}), f32[2048,1536]{1,0:T(8,128)}) %all-gather.7.cloned.1.call-update) | async-done | bytes 12582928 | tf_op jit(solution)/shard_map/all_gather | solution.py:140
  539.3 8.0 reduce_sum.199
  547.3 7.4 multiply_add_fusion.3
  557.3 9.6 convolution_bitcast_fusion.1
  566.8 8.2 fusion.188
  575.0 25.2 %fusion.63 = f32[2048,2,96]{0,2,1:T(8,128)} fusion(bf16[512,2,2,96]{0,3,2,1:T(8,128)(2,1)} %bitcast.495, f32[2,2048,512,2]{2,1,3,0:T(8,128)} %fusion.188, f32[2,2048,512,2]{2,1,3,0:T(8,128)} %copy-done.10, f32[2,2,512]{2,1,0:T(2,128)S(1)} %copy-done.87, pred[512,2048]{0,1:T(8,128)(4,1)} %copy-done.20), kind=kOutput, calls=%fused_computation.113 | convolution fusion | flops 851447808 | bytes 36577280 | tf_op jit(solution)/shard_map/kgqt,qkgd->tkd/dot_general | solution.py:83
  600.3 25.0 %fusion.41 = f32[2,96,2,512]{3,1,2,0:T(8,128)} fusion(f32[2,2048,512,2]{2,1,3,0:T(8,128)} %fusion.188, f32[2,2048,512,2]{2,1,3,0:T(8,128)} %copy-done.10, f32[2,2,512]{2,1,0:T(2,128)S(1)} %copy-done.87, pred[512,2048]{0,1:T(8,128)(4,1)} %copy-done.20, bf16[512,2,96]{0,2,1:T(8,128)(2,1)} %bitcast.534, bf16[512,2,96]{0,2,1:T(8,128)(2,1)} %bitcast.532, ...), kind=kOutput, calls=%fused_computation.87 | convolution fusion | flops 854593536 | bytes 36184064 | tf_op jit(solution)/shard_map/kgqt,tkd->qkgd/dot_general | solution.py:80
  638.7 18.9 collective-permute-done.12
  660.4 5.6 collective-permute-done.13
  666.0 8.4 collective-permute-done.14
  675.5 6.7 collective-permute-done.17
  685.4 86.3 %all-reduce.17.cloned.1.call-done = f32[512,1536]{1,0:T(8,128)} async-done(((f32[512,1536]{1,0:T(8,128)}), f32[512,1536]{1,0:T(8,128)}) %all-reduce.17.cloned.1.call-update) | async-done | bytes 3145744 | tf_op jit(solution)/shard_map/psum | solution.py:234
  780.0 5.1 multiply_convert_fusion.4
  787.0 5.4 convolution_add_fusion.4
  792.5 68.6 %all-reduce.19.cloned.1.call-done = f32[512,1536]{1,0:T(8,128)} async-done(((f32[512,1536]{1,0:T(8,128)}), f32[512,1536]{1,0:T(8,128)}) %all-reduce.19.cloned.1.call-update) | async-done | bytes 3145744 | tf_op jit(solution)/shard_map/psum | solution.py:198
  868.7 9.5 convolution_bitcast_fusion
  878.2 8.1 fusion.189
  886.3 24.6 %fusion.62 = f32[2048,2,96]{0,2,1:T(8,128)} fusion(bf16[512,2,2,96]{0,3,2,1:T(8,128)(2,1)S(1)} %bitcast.493, f32[2,2048,512,2]{2,1,3,0:T(8,128)} %fusion.189, f32[2,2048,512,2]{2,1,3,0:T(8,128)} %copy-done.9, f32[2,2,512]{2,1,0:T(2,128)S(1)} %copy-done.85, pred[512,2048]{0,1:T(8,128)(4,1)S(1)} %copy-done.23), kind=kOutput, calls=%fused_computation.112 | convolution fusion | flops 851447808 | bytes 36577280 | tf_op jit(solution)/shard_map/kgqt,qkgd->tkd/dot_general | solution.py:83
  911.0 23.6 %fusion.44 = f32[2,96,2,512]{3,1,2,0:T(8,128)S(1)} fusion(f32[2,2048,512,2]{2,1,3,0:T(8,128)} %fusion.189, f32[2,2048,512,2]{2,1,3,0:T(8,128)} %copy-done.9, f32[2,2,512]{2,1,0:T(2,128)S(1)} %copy-done.85, pred[512,2048]{0,1:T(8,128)(4,1)S(1)} %copy-done.23, bf16[512,2,96]{0,2,1:T(8,128)(2,1)} %bitcast.14, bf16[512,2,96]{0,2,1:T(8,128)(2,1)} %bitcast.13, ...), kind=kOutput, calls=%fused_computation.90 | convolution fusion | flops 854593536 | bytes 36184064 | tf_op jit(solution)/shard_map/kgqt,tkd->qkgd/dot_general | solution.py:80
  948.2 19.0 collective-permute-done.18
  969.8 5.8 collective-permute-done.19
  975.6 8.4 collective-permute-done.20
  985.1 6.1 collective-permute-done.23
  1003.3 77.7 %all-reduce.21.cloned.1.call-done = f32[512,1536]{1,0:T(8,128)} async-done(((f32[512,1536]{1,0:T(8,128)}), f32[512,1536]{1,0:T(8,128)}) %all-reduce.21.cloned.1.call-update) | async-done | bytes 3145744 | tf_op jit(solution)/shard_map/psum | solution.py:234
  1087.1 4.9 copy.91
  1091.9 4.5 reshape.442
  1101.5 4.8 copy.89
  1106.4 4.5 reshape.440
  1129.6 16.5 copy.64
  1150.4 6.9 copy.63
  1178.5 5.2 multiply_add_fusion
  1183.7 26.8 %reduce-scatter.22.cloned.1.call-done = bf16[192,2]{1,0:T(8,128)(2,1)} async-done(((bf16[1536,2]{1,0:T(8,128)(2,1)}), bf16[192,2]{1,0:T(8,128)(2,1)}) %reduce-scatter.22.cloned.1.call-update) | async-done | bytes 784
  1212.0 65.1 %reduce-scatter.28.cloned.1.call-done = bf16[192,384]{1,0:T(8,128)(2,1)} async-done(((bf16[1536,384]{1,0:T(8,128)(2,1)}), bf16[192,384]{1,0:T(8,128)(2,1)}) %reduce-scatter.28.cloned.1.call-update) | async-done | bytes 147472
  1279.2 64.7 %reduce-scatter.26.cloned.1.call-done = bf16[192,384]{1,0:T(8,128)(2,1)} async-done(((bf16[1536,384]{1,0:T(8,128)(2,1)}), bf16[192,384]{1,0:T(8,128)(2,1)}) %reduce-scatter.26.cloned.1.call-update) | async-done | bytes 147472
  1346.1 69.4 %reduce-scatter.16.cloned.1.call-done = bf16[2,192,384]{2,1,0:T(8,128)(2,1)} async-done(((bf16[2,1536,384]{2,1,0:T(8,128)(2,1)}), bf16[2,192,384]{2,1,0:T(8,128)(2,1)}) %reduce-scatter.16.cloned.1.call-update) | async-done | bytes 294928 | tf_op jit(solution)/shard_map/reduce_scatter | solution.py:332
  1417.3 278.6 %all-reduce.23.cloned.1.call-done = (bf16[2,384,1536]{1,0,2:T(2,128)(2,1)}, bf16[2,1024,1536]{1,0,2:T(2,128)(2,1)}) async-done(((bf16[2,384,1536]{1,0,2:T(2,128)(2,1)}, bf16[2,1024,1536]{1,0,2:T(2,128)(2,1)}), (bf16[2,384,1536]{1,0,2:T(2,128)(2,1)}, bf16[2,1024,1536]{1,0,2:T(2,128)(2,1)})) %all-reduce.23.cloned.1.call-update) | async-done | bytes 8650768
  1701.2 115.5 %reduce-scatter.20.cloned.1.call-done = bf16[2,192,1024]{2,1,0:T(8,128)(2,1)} async-done(((bf16[2,1536,1024]{2,1,0:T(8,128)(2,1)}), bf16[2,192,1024]{2,1,0:T(8,128)(2,1)}) %reduce-scatter.20.cloned.1.call-update) | async-done | bytes 786448 | tf_op jit(solution)/shard_map/reduce_scatter | solution.py:347
  1819.1 118.5 %reduce-scatter.18.cloned.1.call-done = bf16[2,192,1024]{2,1,0:T(8,128)(2,1)} async-done(((bf16[2,1536,1024]{2,1,0:T(8,128)(2,1)}), bf16[2,192,1024]{2,1,0:T(8,128)(2,1)}) %reduce-scatter.18.cloned.1.call-update) | async-done | bytes 786448 | tf_op jit(solution)/shard_map/reduce_scatter | solution.py:344
  (467 shorter events, 260.5 us)
Async XLA Ops:
  7.2 129.7 %all-reduce.11.cloned.1.call-start = ((), (), s32[]{:S(2)}) async-start(), calls=%async_computation.7 | async-start | bytes 6291456 | tf_op jit(solution)/shard_map/psum | solution.py:131
  16.8 19.0 collective-permute-start.3
  19.7 18.7 collective-permute-start.4
  21.3 32.0 %collective-permute-start.5 = (bf16[512,192]{0,1:T(8,128)(2,1)}, bf16[512,192]{0,1:T(8,128)(2,1)}, u32[]{:S(2)}, u32[]{:S(2)}) collective-permute-start(bf16[512,192]{0,1:T(8,128)(2,1)} %bitcast.11), channel_id=1, source_target_pairs={{20,0},{24,4},{28,8},{0,12},{4,16},{8,20},{12,24},{16,28},{21,1},{... | collective-permute-start | bytes 589832 | tf_op jit(solution)/shard_map/ppermute | solution.py:16
  24.6 37.1 %collective-permute-start = (bf16[512,192]{0,1:T(8,128)(2,1)S(1)}, bf16[512,192]{0,1:T(8,128)(2,1)S(1)}, u32[]{:S(2)}, u32[]{:S(2)}) collective-permute-start(bf16[512,192]{0,1:T(8,128)(2,1)S(1)} %convolution_convert_fusion.19), channel_id=1, source_target_pairs={{28,0},{0,4},{4,8},{8,12},{12,16},{16,20},{20,24},{24,28},{29,1},{... | collective-permute-start | bytes 589832 | tf_op jit(solution)/shard_map/ppermute | solution.py:16
  26.1 35.6 %collective-permute-start.1 = (bf16[512,192]{0,1:T(8,128)(2,1)S(1)}, bf16[512,192]{0,1:T(8,128)(2,1)}, u32[]{:S(2)}, u32[]{:S(2)}) collective-permute-start(bf16[512,192]{0,1:T(8,128)(2,1)S(1)} %convolution_convert_fusion.19), channel_id=1, source_target_pairs={{24,0},{28,4},{0,8},{4,12},{8,16},{12,20},{16,24},{20,28},{25,1},{... | collective-permute-start | bytes 589832 | tf_op jit(solution)/shard_map/ppermute | solution.py:16
  35.8 25.9 %collective-permute-start.2 = (bf16[512,192]{0,1:T(8,128)(2,1)S(1)}, bf16[512,192]{0,1:T(8,128)(2,1)S(1)}, u32[]{:S(2)}, u32[]{:S(2)}) collective-permute-start(bf16[512,192]{0,1:T(8,128)(2,1)S(1)} %convolution_convert_fusion.19), channel_id=1, source_target_pairs={{20,0},{24,4},{28,8},{0,12},{4,16},{8,20},{12,24},{16,28},{21,1},{... | collective-permute-start | bytes 589832 | tf_op jit(solution)/shard_map/ppermute | solution.py:16
  71.0 164.4 %all-gather.5.cloned.1.call-start = ((), (), s32[]{:S(2)}) async-start(), calls=%async_computation.16 | async-start | bytes 15728640 | tf_op jit(solution)/shard_map/all_gather | solution.py:140
  72.3 68.0 %copy-start.67 = (f32[1536]{0:T(1024)}, f32[1536]{0:T(1024)S(1)}, u32[]{:S(2)}) copy-start(f32[1536]{0:T(1024)S(1)} %get-tuple-element.53) | copy-start | bytes 18436
  153.0 212.9 %all-reduce.13.cloned.1.call-start = ((), (), s32[]{:S(2)}) async-start(), calls=%async_computation.8 | async-start | bytes 6291456 | tf_op jit(solution)/shard_map/psum | solution.py:131
  248.1 10.6 collective-permute-start.9
  249.6 10.7 collective-permute-start.10
  251.1 32.2 %collective-permute-start.11 = (bf16[512,192]{0,1:T(8,128)(2,1)S(1)}, bf16[512,192]{0,1:T(8,128)(2,1)S(1)}, u32[]{:S(2)}, u32[]{:S(2)}) collective-permute-start(bf16[512,192]{0,1:T(8,128)(2,1)S(1)} %bitcast.510), channel_id=1, source_target_pairs={{20,0},{24,4},{28,8},{0,12},{4,16},{8,20},{12,24},{16,28},{21,1},{... | collective-permute-start | bytes 589832 | tf_op jit(solution)/shard_map/ppermute | solution.py:16
  254.2 35.9 %collective-permute-start.6 = (bf16[512,192]{0,1:T(8,128)(2,1)S(1)}, bf16[512,192]{0,1:T(8,128)(2,1)S(1)}, u32[]{:S(2)}, u32[]{:S(2)}) collective-permute-start(bf16[512,192]{0,1:T(8,128)(2,1)S(1)} %convolution_convert_fusion.18), channel_id=1, source_target_pairs={{28,0},{0,4},{4,8},{8,12},{12,16},{16,20},{20,24},{24,28},{29,1},{... | collective-permute-start | bytes 589832 | tf_op jit(solution)/shard_map/ppermute | solution.py:16
  255.7 34.4 %collective-permute-start.7 = (bf16[512,192]{0,1:T(8,128)(2,1)S(1)}, bf16[512,192]{0,1:T(8,128)(2,1)S(1)}, u32[]{:S(2)}, u32[]{:S(2)}) collective-permute-start(bf16[512,192]{0,1:T(8,128)(2,1)S(1)} %convolution_convert_fusion.18), channel_id=1, source_target_pairs={{24,0},{28,4},{0,8},{4,12},{8,16},{12,20},{16,24},{20,28},{25,1},{... | collective-permute-start | bytes 589832 | tf_op jit(solution)/shard_map/ppermute | solution.py:16
  258.7 31.4 %collective-permute-start.8 = (bf16[512,192]{0,1:T(8,128)(2,1)S(1)}, bf16[512,192]{0,1:T(8,128)(2,1)S(1)}, u32[]{:S(2)}, u32[]{:S(2)}) collective-permute-start(bf16[512,192]{0,1:T(8,128)(2,1)S(1)} %convolution_convert_fusion.18), channel_id=1, source_target_pairs={{20,0},{24,4},{28,8},{0,12},{4,16},{8,20},{12,24},{16,28},{21,1},{... | collective-permute-start | bytes 589832 | tf_op jit(solution)/shard_map/ppermute | solution.py:16
  301.2 68.1 %copy-start.69 = (f32[1536]{0:T(1024)S(1)}, f32[1536]{0:T(1024)}, u32[]{:S(2)}) copy-start(f32[1536]{0:T(1024)} %get-tuple-element.52) | copy-start | bytes 18436
  301.2 154.5 %all-reduce.15.cloned.1.call-start = ((), (), s32[]{:S(2)}) async-start(), calls=%async_computation.9 | async-start | bytes 6291456 | tf_op jit(solution)/shard_map/psum | solution.py:198
  387.0 152.3 %all-gather.7.cloned.1.call-start = ((), (), s32[]{:S(2)}) async-start(), calls=%async_computation.17 | async-start | bytes 15728640 | tf_op jit(solution)/shard_map/all_gather | solution.py:140
  392.7 379.0 %all-reduce.17.cloned.1.call-start = ((), (), s32[]{:S(2)}) async-start(), calls=%async_computation.10 | async-start | bytes 6291456 | tf_op jit(solution)/shard_map/psum | solution.py:234
  627.0 48.6 %collective-permute-start.15 = (f32[512,192]{0,1:T(8,128)S(1)}, f32[512,192]{0,1:T(8,128)S(1)}, u32[]{:S(2)}, u32[]{:S(2)}) collective-permute-start(f32[512,192]{0,1:T(8,128)S(1)} %bitcast.501), channel_id=1, source_target_pairs={{4,0},{8,4},{12,8},{16,12},{20,16},{24,20},{28,24},{0,28},{5,1},{9... | collective-permute-start | bytes 1179656 | tf_op jit(solution)/shard_map/ppermute | solution.py:16
  631.3 44.3 %collective-permute-start.16 = (f32[512,192]{0,1:T(8,128)S(1)}, f32[512,192]{0,1:T(8,128)S(1)}, u32[]{:S(2)}, u32[]{:S(2)}) collective-permute-start(f32[512,192]{0,1:T(8,128)S(1)} %bitcast.499), channel_id=1, source_target_pairs={{8,0},{12,4},{16,8},{20,12},{24,16},{28,20},{0,24},{4,28},{9,1},{1... | collective-permute-start | bytes 1179656 | tf_op jit(solution)/shard_map/ppermute | solution.py:16
  631.9 25.7 %collective-permute-start.12 = (f32[512,192]{0,1:T(8,128)S(1)}, f32[512,192]{0,1:T(8,128)S(1)}, u32[]{:S(2)}, u32[]{:S(2)}) collective-permute-start(f32[512,192]{0,1:T(8,128)S(1)} %bitcast.506), channel_id=1, source_target_pairs={{4,0},{8,4},{12,8},{16,12},{20,16},{24,20},{28,24},{0,28},{5,1},{9... | collective-permute-start | bytes 1179656 | tf_op jit(solution)/shard_map/ppermute | solution.py:16
  632.6 33.5 %collective-permute-start.13 = (f32[512,192]{0,1:T(8,128)S(1)}, f32[512,192]{0,1:T(8,128)S(1)}, u32[]{:S(2)}, u32[]{:S(2)}) collective-permute-start(f32[512,192]{0,1:T(8,128)S(1)} %bitcast.504), channel_id=1, source_target_pairs={{8,0},{12,4},{16,8},{20,12},{24,16},{28,20},{0,24},{4,28},{9,1},{1... | collective-permute-start | bytes 1179656 | tf_op jit(solution)/shard_map/ppermute | solution.py:16
  633.1 41.4 %collective-permute-start.14 = (f32[512,192]{0,1:T(8,128)S(1)}, f32[512,192]{0,1:T(8,128)S(1)}, u32[]{:S(2)}, u32[]{:S(2)}) collective-permute-start(f32[512,192]{0,1:T(8,128)S(1)} %bitcast.502), channel_id=1, source_target_pairs={{12,0},{16,4},{20,8},{24,12},{28,16},{0,20},{4,24},{8,28},{13,1},{... | collective-permute-start | bytes 1179656 | tf_op jit(solution)/shard_map/ppermute | solution.py:16
  657.6 24.6 %collective-permute-start.17 = (f32[512,192]{0,1:T(8,128)S(1)}, f32[512,192]{0,1:T(8,128)S(1)}, u32[]{:S(2)}, u32[]{:S(2)}) collective-permute-start(f32[512,192]{0,1:T(8,128)S(1)} %bitcast.497), channel_id=1, source_target_pairs={{12,0},{16,4},{20,8},{24,12},{28,16},{0,20},{4,24},{8,28},{13,1},{... | collective-permute-start | bytes 1179656 | tf_op jit(solution)/shard_map/ppermute | solution.py:16
  685.3 86.4 %copy-start.78 = (f32[512]{0:T(512)S(1)}, f32[512]{0:T(512)}, u32[]{:S(2)}) copy-start(f32[512]{0:T(512)} %copy-done.77) | copy-start | bytes 6148
  685.3 175.8 %all-reduce.19.cloned.1.call-start = ((), (), s32[]{:S(2)}) async-start(), calls=%async_computation.11 | async-start | bytes 6291456 | tf_op jit(solution)/shard_map/psum | solution.py:198
  792.4 68.7 %copy-start.68 = (f32[1536]{0:T(1024)S(1)}, f32[1536]{0:T(1024)}, u32[]{:S(2)}) copy-start(f32[1536]{0:T(1024)} %copy-done.67) | copy-start | bytes 18436
  792.4 68.7 %copy-start.76 = (f32[512]{0:T(512)S(1)}, f32[512]{0:T(512)}, u32[]{:S(2)}) copy-start(f32[512]{0:T(512)} %copy-done.75) | copy-start | bytes 6148
  792.4 288.6 %all-reduce.21.cloned.1.call-start = ((), (), s32[]{:S(2)}) async-start(), calls=%async_computation.12 | async-start | bytes 6291456 | tf_op jit(solution)/shard_map/psum | solution.py:234
  936.5 48.6 %collective-permute-start.21 = (f32[512,192]{0,1:T(8,128)S(1)}, f32[512,192]{0,1:T(8,128)S(1)}, u32[]{:S(2)}, u32[]{:S(2)}) collective-permute-start(f32[512,192]{0,1:T(8,128)S(1)} %bitcast.500), channel_id=1, source_target_pairs={{4,0},{8,4},{12,8},{16,12},{20,16},{24,20},{28,24},{0,28},{5,1},{9... | collective-permute-start | bytes 1179656 | tf_op jit(solution)/shard_map/ppermute | solution.py:16
  940.8 44.4 %collective-permute-start.22 = (f32[512,192]{0,1:T(8,128)S(1)}, f32[512,192]{0,1:T(8,128)S(1)}, u32[]{:S(2)}, u32[]{:S(2)}) collective-permute-start(f32[512,192]{0,1:T(8,128)S(1)} %bitcast.498), channel_id=1, source_target_pairs={{8,0},{12,4},{16,8},{20,12},{24,16},{28,20},{0,24},{4,28},{9,1},{1... | collective-permute-start | bytes 1179656 | tf_op jit(solution)/shard_map/ppermute | solution.py:16
  941.4 25.7 %collective-permute-start.18 = (f32[512,192]{0,1:T(8,128)S(1)}, f32[512,192]{0,1:T(8,128)S(1)}, u32[]{:S(2)}, u32[]{:S(2)}) collective-permute-start(f32[512,192]{0,1:T(8,128)S(1)} %bitcast.507), channel_id=1, source_target_pairs={{4,0},{8,4},{12,8},{16,12},{20,16},{24,20},{28,24},{0,28},{5,1},{9... | collective-permute-start | bytes 1179656 | tf_op jit(solution)/shard_map/ppermute | solution.py:16
  942.1 33.6 %collective-permute-start.19 = (f32[512,192]{0,1:T(8,128)S(1)}, f32[512,192]{0,1:T(8,128)S(1)}, u32[]{:S(2)}, u32[]{:S(2)}) collective-permute-start(f32[512,192]{0,1:T(8,128)S(1)} %bitcast.505), channel_id=1, source_target_pairs={{8,0},{12,4},{16,8},{20,12},{24,16},{28,20},{0,24},{4,28},{9,1},{1... | collective-permute-start | bytes 1179656 | tf_op jit(solution)/shard_map/ppermute | solution.py:16
  942.6 41.4 %collective-permute-start.20 = (f32[512,192]{0,1:T(8,128)S(1)}, f32[512,192]{0,1:T(8,128)S(1)}, u32[]{:S(2)}, u32[]{:S(2)}) collective-permute-start(f32[512,192]{0,1:T(8,128)S(1)} %bitcast.503), channel_id=1, source_target_pairs={{12,0},{16,4},{20,8},{24,12},{28,16},{0,20},{4,24},{8,28},{13,1},{... | collective-permute-start | bytes 1179656 | tf_op jit(solution)/shard_map/ppermute | solution.py:16
  967.2 24.0 %collective-permute-start.23 = (f32[512,192]{0,1:T(8,128)S(1)}, f32[512,192]{0,1:T(8,128)S(1)}, u32[]{:S(2)}, u32[]{:S(2)}) collective-permute-start(f32[512,192]{0,1:T(8,128)S(1)} %bitcast.496), channel_id=1, source_target_pairs={{12,0},{16,4},{20,8},{24,12},{28,16},{0,20},{4,24},{8,28},{13,1},{... | collective-permute-start | bytes 1179656 | tf_op jit(solution)/shard_map/ppermute | solution.py:16
  994.3 86.7 %copy-start.3 = (f32[512,1536]{1,0:T(8,128)S(1)}, f32[512,1536]{1,0:T(8,128)}, u32[]{:S(2)}) copy-start(f32[512,1536]{1,0:T(8,128)} %param.12) | copy-start | bytes 9437188
  994.3 86.7 %copy-start.66 = (f32[1536]{0:T(1024)S(1)}, f32[1536]{0:T(1024)}, u32[]{:S(2)}) copy-start(f32[1536]{0:T(1024)} %copy-done.65) | copy-start | bytes 18436
  994.3 86.7 %copy-start.74 = (f32[512]{0:T(512)S(1)}, f32[512]{0:T(512)}, u32[]{:S(2)}) copy-start(f32[512]{0:T(512)} %copy-done.73) | copy-start | bytes 6148
  994.3 182.7 %reduce-scatter.24.cloned.1.call-start = ((), (), s32[]{:S(2)}) async-start(), calls=%async_computation.19 | async-start | bytes 442368
  1000.4 210.1 %reduce-scatter.22.cloned.1.call-start = ((), (), s32[]{:S(2)}) async-start(), calls=%async_computation.18 | async-start | bytes 442368
  1084.6 192.4 %reduce-scatter.28.cloned.1.call-start = ((), (), s32[]{:S(2)}) async-start(), calls=%async_computation.21 | async-start | bytes 1327104
  1096.4 247.5 %reduce-scatter.26.cloned.1.call-start = ((), (), s32[]{:S(2)}) async-start(), calls=%async_computation.20 | async-start | bytes 1327104
  1110.9 304.6 %reduce-scatter.16.cloned.1.call-start = ((), (), s32[]{:S(2)}) async-start(), calls=%async_computation.13 | async-start | bytes 2654208 | tf_op jit(solution)/shard_map/reduce_scatter | solution.py:332
  1117.1 578.7 %all-reduce.23.cloned.1.call-start = ((), (), s32[]{:S(2)}) async-start(), calls=%async_computation.22 | async-start | bytes 17301504
  1157.3 659.3 %reduce-scatter.20.cloned.1.call-start = ((), (), s32[]{:S(2)}) async-start(), calls=%async_computation.15 | async-start | bytes 7077888 | tf_op jit(solution)/shard_map/reduce_scatter | solution.py:347
  1166.1 771.5 %reduce-scatter.18.cloned.1.call-start = ((), (), s32[]{:S(2)}) async-start(), calls=%async_computation.14 | async-start | bytes 7077888 | tf_op jit(solution)/shard_map/reduce_scatter | solution.py:344
  (110 other events, 737.2 us)
Sparse Core Ops, SparseCore 0:
  71.1 65.7 all-reduce.10
  153.1 82.1 all-gather.4
  301.3 64.5 all-reduce.12
  387.1 68.5 all-reduce.14
  457.1 82.1 all-gather.6
  685.5 86.1 all-reduce.16
  792.5 68.5 all-reduce.18
  994.4 86.5 all-reduce.20
  1084.8 61.5 reduce-scatter.23
  1150.1 60.4 reduce-scatter.21
  1213.9 63.1 reduce-scatter.27
  1280.9 63.0 reduce-scatter.25
  1347.4 67.9 reduce-scatter.15
  1419.3 276.4 all-reduce.22
  1699.7 116.9 reduce-scatter.19
  1820.5 117.0 reduce-scatter.17
